TPU v7x, 32 devices: a whole 2x2x4 slice. The times are simulated.
32 devices in a mesh: blk: 8 (over z, y), labels: 4 (over x, core).
Axes of the slice: x: 2, y: 2, z: 4, core: 2. Of those that a mesh axis runs over, the one named last changes fastest.
Arguments:
- features: bfloat16 [6144, 4096], P('blk'), may hold values from -0.099609375 to 0.099609375
- positives: int32 [6144, 8], P('blk'), may hold values from 0 to 16383
- tile_rows: int32 [128, 4], P(('labels', 'blk')), may hold values from 0 to 31, as said below
- tile_count: int32 [128], P(('labels', 'blk')), may hold values from 1 to 4, as said below
- weight: float32 [128, 4, 128, 128], P(('labels', 'blk')), may hold values from -96 to 96
- first_moment: float32 [128, 4, 128, 128], P(('labels', 'blk')), may hold values from -3 to 3
- second_moment: float32 [128, 4, 128, 128], P(('labels', 'blk')), may hold values from 0.05 to 2
Outputs:
- new_weight: float32 [128, 4, 128, 128], P(('labels', 'blk'))
- new_first: float32 [128, 4, 128, 128], P(('labels', 'blk'))
- new_second: float32 [128, 4, 128, 128], P(('labels', 'blk'))
Inputs may be any that keep to these rules, and one draw needn't show every extreme that they name: `tile_rows`: in each column block the 4 entries are distinct tile rows; only the first tile_count entries name kept tiles. `tile_count`: every column block keeps at least one tile.
All inputs are finite; a program needn't handle non-finite values.
Results may differ from a plain program's by a relative error of at most 0.0003.
Values may be sent and summed in bfloat16 or wider, within the bound.
A program may use at most 64 MiB of HBM per device.

v0:
```python
import jax
import jax.numpy as jnp
from jax import lax
from jax.sharding import PartitionSpec as P

beta_one = 0.9
beta_two = 0.999
adam_eps = 1e-08
learn_rate = 0.1
correction_one = 1.0 - 0.9**10
correction_two = 1.0 - 0.999**10


def from_behind(array, axis, by):
    devices = lax.axis_size(axis)
    return lax.ppermute(array, axis, [(i, (i + by) % devices) for i in range(devices)])


def tile_residual(chosen, positives, block_count, block_tiles, block_base):
    tile_side = block_tiles.shape[-1]
    slot_ids = jnp.arange(block_tiles.shape[0], dtype=jnp.int32)
    live_mask = slot_ids < block_count
    w_masked = jnp.where(live_mask[:, None, None], block_tiles, jnp.zeros_like(block_tiles))
    logits = jnp.einsum("rsk,skt->rt", chosen, w_masked, preferred_element_type=jnp.float32)
    label_ids = block_base + jnp.arange(tile_side, dtype=jnp.int32)
    targets = jnp.any(positives[:, :, None] == label_ids[None, None, :], axis=1).astype(jnp.float32)
    return (jax.nn.sigmoid(logits) - targets).astype(jnp.bfloat16)


def block_both(tile_split, positives, row_ids, slot_counts, tiles_now, label_base):

    def one_block(block_args):
        block_rows, block_count, block_tiles, block_base = block_args
        chosen = jnp.take(tile_split, block_rows, axis=1)
        block_resid = tile_residual(chosen, positives, block_count, block_tiles, block_base)
        return jnp.einsum("rsk,rt->skt", chosen, block_resid, preferred_element_type=jnp.float32)

    return lax.map(one_block, (row_ids, slot_counts, tiles_now, label_base))


def local(features, positives, tile_rows, tile_count, weight, first_moment, second_moment):
    own_blocks = weight.shape[0]
    tile_side = weight.shape[-1]
    row_total = features.shape[0]
    tile_split = features.reshape(row_total, features.shape[1] // tile_side, tile_side)
    all_rows, all_counts = (
        lax.all_gather(tile_rows, "blk", axis=0, tiled=True),
        lax.all_gather(tile_count, "blk", axis=0, tiled=True),
    )
    group_blocks = all_rows.shape[0]
    group_base = lax.axis_index("labels") * (group_blocks * tile_side)
    tiles_half = weight.astype(jnp.bfloat16)

    def slice_index(first_row, block_total):
        row_ids = lax.dynamic_slice_in_dim(all_rows, first_row, block_total, 0)
        slot_counts = lax.dynamic_slice_in_dim(all_counts, first_row, block_total, 0)
        label_base = group_base + (first_row + jnp.arange(block_total, dtype=jnp.int32)) * tile_side
        return (row_ids, slot_counts, label_base)

    cycle_pos = lax.axis_index("blk")
    cycle_size = lax.axis_size("blk")

    def turn(turn_idx, loop_state):
        tiles_now, accumulated = loop_state
        owner_idx = jnp.mod(cycle_pos - turn_idx, cycle_size)
        first_row = owner_idx * own_blocks
        row_ids, slot_counts, label_base = slice_index(first_row, own_blocks)
        accumulated = accumulated + block_both(
            tile_split, positives, row_ids, slot_counts, tiles_now, label_base
        )
        tiles_now = from_behind(tiles_now, "blk", 1)
        accumulated = from_behind(accumulated, "blk", 1)
        return (tiles_now, accumulated)

    start_acc = jnp.zeros(weight.shape, jnp.float32)
    _, gradient = lax.fori_loop(0, cycle_size, turn, (tiles_half, start_acc))
    slot_ids = jnp.arange(weight.shape[1], dtype=jnp.int32)
    kept = (slot_ids[None, :] < tile_count[:, None])[:, :, None, None]
    moved_first = beta_one * first_moment + (1.0 - beta_one) * gradient
    moved_second = beta_two * second_moment + (1.0 - beta_two) * gradient * gradient
    step_dir = moved_first / correction_one / (jnp.sqrt(moved_second / correction_two) + adam_eps)
    moved_weight = weight - learn_rate * step_dir
    new_weight = jnp.where(kept, moved_weight, weight)
    new_first = jnp.where(kept, moved_first, first_moment)
    new_second = jnp.where(kept, moved_second, second_moment)
    return (new_weight, new_first, new_second)


def solution(mesh):
    return jax.shard_map(
        local,
        mesh=mesh,
        in_specs=(
            P("blk", None),
            P("blk", None),
            P(("labels", "blk"), None),
            P(("labels", "blk")),
            P(("labels", "blk"), None, None, None),
            P(("labels", "blk"), None, None, None),
            P(("labels", "blk"), None, None, None),
        ),
        out_specs=(
            P(("labels", "blk"), None, None, None),
            P(("labels", "blk"), None, None, None),
            P(("labels", "blk"), None, None, None),
        ),
        check_vma=False,
    )
```

profile of v0, /device:TPU:8, one launch (start us, length us, event | category | flops | bytes accessed | tf_op | source)
XLA Modules:
  0.0 689.8 jit_solution(7104321564340805829)
XLA Ops:
  3.4 10.5 %all-reduce = s32[32]{0:T(128)S(1)} all-reduce(s32[32]{0:T(128)S(1)} %dynamic-update-slice), channel_id=1, replica_groups=mesh['blk'=8,'labels'=4] {'blk'}, use_global_device_ids=true, to_apply=%add | all-reduce | flops 32 | bytes 256
  13.9 8.6 %copy.32 = bf16[768,4096]{0,1:T(8,128)(2,1)} copy(bf16[768,4096]{1,0:T(8,128)(2,1)} %param.11) | data formatting | bytes 12582912 | tf_op args[0]
  22.5 8.7 %copy.34 = bf16[768,32,128]{2,0,1:T(8,128)(2,1)} copy(bf16[768,32,128]{0,2,1:T(8,128)(2,1)} %bitcast.68) | data formatting | bytes 12582912 | tf_op jit(solution)/shard_map/while | solution.py:76
  31.5 25.9 %all-gather = s32[8,4,4]{2,1,0:T(4,128)S(1)} all-gather(s32[1,4,4]{2,1,0:T(4,128)S(1)} %bitcast.70), channel_id=1, replica_groups=mesh['blk'=8,'labels'=4] {'blk'}, dimensions={0}, use_global_device_ids=true | all-gather | bytes 576 | tf_op jit(solution)/shard_map/all_gather | solution.py:47
  57.6 627.7 %while.49 = (s32[]{:T(128)}, bf16[4,4,128,128]{3,2,1,0:T(8,128)(2,1)S(1)}, f32[4,4,128,128]{3,2,1,0:T(8,128)S(1)}, s32[]{:T(128)}, s32[32,4]{1,0:T(8,128)S(1)}, ...) while((s32[]{:T(128)}, ...), condition=%wide.region_4.5_spmd, body=%wide.region_0.4_spmd.sunk | while | flops 204506320 | bytes 14254457 | solution.py:76
  58.5 48.6 %while.50 = (s32[]{:T(128)}, f32[4,4,128,128]{3,2,1,0:T(8,128)S(1)}, s32[4,4]{1,0:T(4,128)S(1)}, bf16[768,32,128]{2,0,1:T(8,128)(2,1)}, s32[4]{0:T(128)S(1)}, /*...) while((s32[]{:T(128)}, f32[4,4,128,128]{3,2,1,0:T(8,128)S(1)}, ...), condition=%wide.region_3.3_spmd, body=%wide.region_1.2_spmd.sunk | while | flops 204244144 | bytes 3768029 | solution.py:38
  89.1 3.9 compare_reduce_fusion.2
  101.2 3.9 compare_reduce_fusion.2
  109.9 27.4 %collective-permute-done = bf16[4,4,128,128]{3,2,1,0:T(8,128)(2,1)S(1)} collective-permute-done((bf16[4,4,128,128]{3,2,1,0:T(8,128)(2,1)}, bf16[4,4,128,128]{3,2,1,0:T(8,128)(2,1)S(1)}, u32[]{:S(2)}, u32[]{:S(2)}) %collective-permute-start) | collective-permute-done | bytes 524320 | tf_op jit(solution)/shard_map/while/body/eval_jaxpr/ppermute | solution.py:16
  138.2 48.6 %while.50 = (s32[]{:T(128)}, f32[4,4,128,128]{3,2,1,0:T(8,128)S(1)}, s32[4,4]{1,0:T(4,128)S(1)}, bf16[768,32,128]{2,0,1:T(8,128)(2,1)}, s32[4]{0:T(128)S(1)}, /*...) while((s32[]{:T(128)}, f32[4,4,128,128]{3,2,1,0:T(8,128)S(1)}, ...), condition=%wide.region_3.3_spmd, body=%wide.region_1.2_spmd.sunk | while | flops 204244144 | bytes 3768029 | solution.py:38
  189.1 27.2 %collective-permute-done = bf16[4,4,128,128]{3,2,1,0:T(8,128)(2,1)S(1)} collective-permute-done((bf16[4,4,128,128]{3,2,1,0:T(8,128)(2,1)}, bf16[4,4,128,128]{3,2,1,0:T(8,128)(2,1)S(1)}, u32[]{:S(2)}, u32[]{:S(2)}) %collective-permute-start) | collective-permute-done | bytes 524320 | tf_op jit(solution)/shard_map/while/body/eval_jaxpr/ppermute | solution.py:16
  217.1 48.6 %while.50 = (s32[]{:T(128)}, f32[4,4,128,128]{3,2,1,0:T(8,128)S(1)}, s32[4,4]{1,0:T(4,128)S(1)}, bf16[768,32,128]{2,0,1:T(8,128)(2,1)}, s32[4]{0:T(128)S(1)}, /*...) while((s32[]{:T(128)}, f32[4,4,128,128]{3,2,1,0:T(8,128)S(1)}, ...), condition=%wide.region_3.3_spmd, body=%wide.region_1.2_spmd.sunk | while | flops 204244144 | bytes 3768029 | solution.py:38
  267.4 28.7 %collective-permute-done = bf16[4,4,128,128]{3,2,1,0:T(8,128)(2,1)S(1)} collective-permute-done((bf16[4,4,128,128]{3,2,1,0:T(8,128)(2,1)}, bf16[4,4,128,128]{3,2,1,0:T(8,128)(2,1)S(1)}, u32[]{:S(2)}, u32[]{:S(2)}) %collective-permute-start) | collective-permute-done | bytes 524320 | tf_op jit(solution)/shard_map/while/body/eval_jaxpr/ppermute | solution.py:16
  296.9 48.6 %while.50 = (s32[]{:T(128)}, f32[4,4,128,128]{3,2,1,0:T(8,128)S(1)}, s32[4,4]{1,0:T(4,128)S(1)}, bf16[768,32,128]{2,0,1:T(8,128)(2,1)}, s32[4]{0:T(128)S(1)}, /*...) while((s32[]{:T(128)}, f32[4,4,128,128]{3,2,1,0:T(8,128)S(1)}, ...), condition=%wide.region_3.3_spmd, body=%wide.region_1.2_spmd.sunk | while | flops 204244144 | bytes 3768029 | solution.py:38
  346.6 29.0 %collective-permute-done = bf16[4,4,128,128]{3,2,1,0:T(8,128)(2,1)S(1)} collective-permute-done((bf16[4,4,128,128]{3,2,1,0:T(8,128)(2,1)}, bf16[4,4,128,128]{3,2,1,0:T(8,128)(2,1)S(1)}, u32[]{:S(2)}, u32[]{:S(2)}) %collective-permute-start) | collective-permute-done | bytes 524320 | tf_op jit(solution)/shard_map/while/body/eval_jaxpr/ppermute | solution.py:16
  376.5 48.6 %while.50 = (s32[]{:T(128)}, f32[4,4,128,128]{3,2,1,0:T(8,128)S(1)}, s32[4,4]{1,0:T(4,128)S(1)}, bf16[768,32,128]{2,0,1:T(8,128)(2,1)}, s32[4]{0:T(128)S(1)}, /*...) while((s32[]{:T(128)}, f32[4,4,128,128]{3,2,1,0:T(8,128)S(1)}, ...), condition=%wide.region_3.3_spmd, body=%wide.region_1.2_spmd.sunk | while | flops 204244144 | bytes 3768029 | solution.py:38
  426.2 28.1 %collective-permute-done = bf16[4,4,128,128]{3,2,1,0:T(8,128)(2,1)S(1)} collective-permute-done((bf16[4,4,128,128]{3,2,1,0:T(8,128)(2,1)}, bf16[4,4,128,128]{3,2,1,0:T(8,128)(2,1)S(1)}, u32[]{:S(2)}, u32[]{:S(2)}) %collective-permute-start) | collective-permute-done | bytes 524320 | tf_op jit(solution)/shard_map/while/body/eval_jaxpr/ppermute | solution.py:16
  455.2 48.6 %while.50 = (s32[]{:T(128)}, f32[4,4,128,128]{3,2,1,0:T(8,128)S(1)}, s32[4,4]{1,0:T(4,128)S(1)}, bf16[768,32,128]{2,0,1:T(8,128)(2,1)}, s32[4]{0:T(128)S(1)}, /*...) while((s32[]{:T(128)}, f32[4,4,128,128]{3,2,1,0:T(8,128)S(1)}, ...), condition=%wide.region_3.3_spmd, body=%wide.region_1.2_spmd.sunk | while | flops 204244144 | bytes 3768029 | solution.py:38
  504.9 27.3 %collective-permute-done = bf16[4,4,128,128]{3,2,1,0:T(8,128)(2,1)S(1)} collective-permute-done((bf16[4,4,128,128]{3,2,1,0:T(8,128)(2,1)}, bf16[4,4,128,128]{3,2,1,0:T(8,128)(2,1)S(1)}, u32[]{:S(2)}, u32[]{:S(2)}) %collective-permute-start) | collective-permute-done | bytes 524320 | tf_op jit(solution)/shard_map/while/body/eval_jaxpr/ppermute | solution.py:16
  533.0 48.6 %while.50 = (s32[]{:T(128)}, f32[4,4,128,128]{3,2,1,0:T(8,128)S(1)}, s32[4,4]{1,0:T(4,128)S(1)}, bf16[768,32,128]{2,0,1:T(8,128)(2,1)}, s32[4]{0:T(128)S(1)}, /*...) while((s32[]{:T(128)}, f32[4,4,128,128]{3,2,1,0:T(8,128)S(1)}, ...), condition=%wide.region_3.3_spmd, body=%wide.region_1.2_spmd.sunk | while | flops 204244144 | bytes 3768029 | solution.py:38
  582.7 26.4 %collective-permute-done = bf16[4,4,128,128]{3,2,1,0:T(8,128)(2,1)S(1)} collective-permute-done((bf16[4,4,128,128]{3,2,1,0:T(8,128)(2,1)}, bf16[4,4,128,128]{3,2,1,0:T(8,128)(2,1)S(1)}, u32[]{:S(2)}, u32[]{:S(2)}) %collective-permute-start) | collective-permute-done | bytes 524320 | tf_op jit(solution)/shard_map/while/body/eval_jaxpr/ppermute | solution.py:16
  610.0 48.6 %while.50 = (s32[]{:T(128)}, f32[4,4,128,128]{3,2,1,0:T(8,128)S(1)}, s32[4,4]{1,0:T(4,128)S(1)}, bf16[768,32,128]{2,0,1:T(8,128)(2,1)}, s32[4]{0:T(128)S(1)}, /*...) while((s32[]{:T(128)}, f32[4,4,128,128]{3,2,1,0:T(8,128)S(1)}, ...), condition=%wide.region_3.3_spmd, body=%wide.region_1.2_spmd.sunk | while | flops 204244144 | bytes 3768029 | solution.py:38
  659.7 25.5 %collective-permute-done = bf16[4,4,128,128]{3,2,1,0:T(8,128)(2,1)S(1)} collective-permute-done((bf16[4,4,128,128]{3,2,1,0:T(8,128)(2,1)}, bf16[4,4,128,128]{3,2,1,0:T(8,128)(2,1)S(1)}, u32[]{:S(2)}, u32[]{:S(2)}) %collective-permute-start) | collective-permute-done | bytes 524320 | tf_op jit(solution)/shard_map/while/body/eval_jaxpr/ppermute | solution.py:16
  685.3 4.5 fusion.34
  (373 shorter events, 400.5 us)
Async XLA Ops:
  22.5 8.7 %copy-start = (f32[4,4,128,128]{3,2,1,0:T(8,128)S(1)}, f32[4,4,128,128]{3,2,1,0:T(8,128)}, u32[]{:S(2)}) copy-start(f32[4,4,128,128]{3,2,1,0:T(8,128)} %param.15) | copy-start | bytes 3145732
  22.5 8.8 %copy-start.1 = (s32[768,8]{0,1:T(8,128)S(1)}, s32[768,8]{0,1:T(8,128)}, u32[]{:S(2)}) copy-start(s32[768,8]{0,1:T(8,128)} %param.12) | copy-start | bytes 73732
  22.5 9.0 %copy-start.2 = (s32[4,4]{1,0:T(4,128)S(1)}, s32[4,4]{1,0:T(4,128)}, u32[]{:S(2)}) copy-start(s32[4,4]{1,0:T(4,128)} %param.13) | copy-start | bytes 196
  57.5 627.7 %copy-start.3 = (s32[4]{0:T(128)S(1)}, s32[4]{0:T(128)}, u32[]{:S(2)}) copy-start(s32[4]{0:T(128)} %param.14) | copy-start | bytes 52
  108.2 29.2 %collective-permute-start.1 = (f32[4,4,128,128]{3,2,1,0:T(8,128)}, f32[4,4,128,128]{3,2,1,0:T(8,128)S(1)}, u32[]{:S(2)}, u32[]{:S(2)}) collective-permute-start(f32[4,4,128,128]{3,2,1,0:T(8,128)} %add.197), channel_id=1, source_target_pairs={{0,4},{4,8},{8,12},{12,16},{16,20},{20,24},{24,28},{28,0},{1,5},{5... | collective-permute-start | bytes 3145736 | tf_op jit(solution)/shard_map/while/body/eval_jaxpr/ppermute | solution.py:16
  108.2 29.2 %collective-permute-start = (bf16[4,4,128,128]{3,2,1,0:T(8,128)(2,1)}, bf16[4,4,128,128]{3,2,1,0:T(8,128)(2,1)S(1)}, u32[]{:S(2)}, u32[]{:S(2)}) collective-permute-start(bf16[4,4,128,128]{3,2,1,0:T(8,128)(2,1)} %get-tuple-element.557), channel_id=1, source_target_pairs={{0,4},{4,8},{8,12},{12,16},{16,20},{20,24},{24,28},{28,0},{1,5},{5... | collective-permute-start | bytes 1572872 | tf_op jit(solution)/shard_map/while/body/eval_jaxpr/ppermute | solution.py:16
  187.9 28.3 %collective-permute-start.1 = (f32[4,4,128,128]{3,2,1,0:T(8,128)}, f32[4,4,128,128]{3,2,1,0:T(8,128)S(1)}, u32[]{:S(2)}, u32[]{:S(2)}) collective-permute-start(f32[4,4,128,128]{3,2,1,0:T(8,128)} %add.197), channel_id=1, source_target_pairs={{0,4},{4,8},{8,12},{12,16},{16,20},{20,24},{24,28},{28,0},{1,5},{5... | collective-permute-start | bytes 3145736 | tf_op jit(solution)/shard_map/while/body/eval_jaxpr/ppermute | solution.py:16
  187.9 28.3 %collective-permute-start = (bf16[4,4,128,128]{3,2,1,0:T(8,128)(2,1)}, bf16[4,4,128,128]{3,2,1,0:T(8,128)(2,1)S(1)}, u32[]{:S(2)}, u32[]{:S(2)}) collective-permute-start(bf16[4,4,128,128]{3,2,1,0:T(8,128)(2,1)} %get-tuple-element.557), channel_id=1, source_target_pairs={{0,4},{4,8},{8,12},{12,16},{16,20},{20,24},{24,28},{28,0},{1,5},{5... | collective-permute-start | bytes 1572872 | tf_op jit(solution)/shard_map/while/body/eval_jaxpr/ppermute | solution.py:16
  266.8 29.2 %collective-permute-start.1 = (f32[4,4,128,128]{3,2,1,0:T(8,128)}, f32[4,4,128,128]{3,2,1,0:T(8,128)S(1)}, u32[]{:S(2)}, u32[]{:S(2)}) collective-permute-start(f32[4,4,128,128]{3,2,1,0:T(8,128)} %add.197), channel_id=1, source_target_pairs={{0,4},{4,8},{8,12},{12,16},{16,20},{20,24},{24,28},{28,0},{1,5},{5... | collective-permute-start | bytes 3145736 | tf_op jit(solution)/shard_map/while/body/eval_jaxpr/ppermute | solution.py:16
  266.8 29.2 %collective-permute-start = (bf16[4,4,128,128]{3,2,1,0:T(8,128)(2,1)}, bf16[4,4,128,128]{3,2,1,0:T(8,128)(2,1)S(1)}, u32[]{:S(2)}, u32[]{:S(2)}) collective-permute-start(bf16[4,4,128,128]{3,2,1,0:T(8,128)(2,1)} %get-tuple-element.557), channel_id=1, source_target_pairs={{0,4},{4,8},{8,12},{12,16},{16,20},{20,24},{24,28},{28,0},{1,5},{5... | collective-permute-start | bytes 1572872 | tf_op jit(solution)/shard_map/while/body/eval_jaxpr/ppermute | solution.py:16
  346.6 29.0 %collective-permute-start.1 = (f32[4,4,128,128]{3,2,1,0:T(8,128)}, f32[4,4,128,128]{3,2,1,0:T(8,128)S(1)}, u32[]{:S(2)}, u32[]{:S(2)}) collective-permute-start(f32[4,4,128,128]{3,2,1,0:T(8,128)} %add.197), channel_id=1, source_target_pairs={{0,4},{4,8},{8,12},{12,16},{16,20},{20,24},{24,28},{28,0},{1,5},{5... | collective-permute-start | bytes 3145736 | tf_op jit(solution)/shard_map/while/body/eval_jaxpr/ppermute | solution.py:16
  346.6 29.0 %collective-permute-start = (bf16[4,4,128,128]{3,2,1,0:T(8,128)(2,1)}, bf16[4,4,128,128]{3,2,1,0:T(8,128)(2,1)S(1)}, u32[]{:S(2)}, u32[]{:S(2)}) collective-permute-start(bf16[4,4,128,128]{3,2,1,0:T(8,128)(2,1)} %get-tuple-element.557), channel_id=1, source_target_pairs={{0,4},{4,8},{8,12},{12,16},{16,20},{20,24},{24,28},{28,0},{1,5},{5... | collective-permute-start | bytes 1572872 | tf_op jit(solution)/shard_map/while/body/eval_jaxpr/ppermute | solution.py:16
  426.2 28.1 %collective-permute-start.1 = (f32[4,4,128,128]{3,2,1,0:T(8,128)}, f32[4,4,128,128]{3,2,1,0:T(8,128)S(1)}, u32[]{:S(2)}, u32[]{:S(2)}) collective-permute-start(f32[4,4,128,128]{3,2,1,0:T(8,128)} %add.197), channel_id=1, source_target_pairs={{0,4},{4,8},{8,12},{12,16},{16,20},{20,24},{24,28},{28,0},{1,5},{5... | collective-permute-start | bytes 3145736 | tf_op jit(solution)/shard_map/while/body/eval_jaxpr/ppermute | solution.py:16
  426.2 28.1 %collective-permute-start = (bf16[4,4,128,128]{3,2,1,0:T(8,128)(2,1)}, bf16[4,4,128,128]{3,2,1,0:T(8,128)(2,1)S(1)}, u32[]{:S(2)}, u32[]{:S(2)}) collective-permute-start(bf16[4,4,128,128]{3,2,1,0:T(8,128)(2,1)} %get-tuple-element.557), channel_id=1, source_target_pairs={{0,4},{4,8},{8,12},{12,16},{16,20},{20,24},{24,28},{28,0},{1,5},{5... | collective-permute-start | bytes 1572872 | tf_op jit(solution)/shard_map/while/body/eval_jaxpr/ppermute | solution.py:16
  504.9 27.3 %collective-permute-start.1 = (f32[4,4,128,128]{3,2,1,0:T(8,128)}, f32[4,4,128,128]{3,2,1,0:T(8,128)S(1)}, u32[]{:S(2)}, u32[]{:S(2)}) collective-permute-start(f32[4,4,128,128]{3,2,1,0:T(8,128)} %add.197), channel_id=1, source_target_pairs={{0,4},{4,8},{8,12},{12,16},{16,20},{20,24},{24,28},{28,0},{1,5},{5... | collective-permute-start | bytes 3145736 | tf_op jit(solution)/shard_map/while/body/eval_jaxpr/ppermute | solution.py:16
  504.9 27.3 %collective-permute-start = (bf16[4,4,128,128]{3,2,1,0:T(8,128)(2,1)}, bf16[4,4,128,128]{3,2,1,0:T(8,128)(2,1)S(1)}, u32[]{:S(2)}, u32[]{:S(2)}) collective-permute-start(bf16[4,4,128,128]{3,2,1,0:T(8,128)(2,1)} %get-tuple-element.557), channel_id=1, source_target_pairs={{0,4},{4,8},{8,12},{12,16},{16,20},{20,24},{24,28},{28,0},{1,5},{5... | collective-permute-start | bytes 1572872 | tf_op jit(solution)/shard_map/while/body/eval_jaxpr/ppermute | solution.py:16
  582.7 26.4 %collective-permute-start.1 = (f32[4,4,128,128]{3,2,1,0:T(8,128)}, f32[4,4,128,128]{3,2,1,0:T(8,128)S(1)}, u32[]{:S(2)}, u32[]{:S(2)}) collective-permute-start(f32[4,4,128,128]{3,2,1,0:T(8,128)} %add.197), channel_id=1, source_target_pairs={{0,4},{4,8},{8,12},{12,16},{16,20},{20,24},{24,28},{28,0},{1,5},{5... | collective-permute-start | bytes 3145736 | tf_op jit(solution)/shard_map/while/body/eval_jaxpr/ppermute | solution.py:16
  582.7 26.4 %collective-permute-start = (bf16[4,4,128,128]{3,2,1,0:T(8,128)(2,1)}, bf16[4,4,128,128]{3,2,1,0:T(8,128)(2,1)S(1)}, u32[]{:S(2)}, u32[]{:S(2)}) collective-permute-start(bf16[4,4,128,128]{3,2,1,0:T(8,128)(2,1)} %get-tuple-element.557), channel_id=1, source_target_pairs={{0,4},{4,8},{8,12},{12,16},{16,20},{20,24},{24,28},{28,0},{1,5},{5... | collective-permute-start | bytes 1572872 | tf_op jit(solution)/shard_map/while/body/eval_jaxpr/ppermute | solution.py:16
  659.7 25.5 %collective-permute-start.1 = (f32[4,4,128,128]{3,2,1,0:T(8,128)}, f32[4,4,128,128]{3,2,1,0:T(8,128)S(1)}, u32[]{:S(2)}, u32[]{:S(2)}) collective-permute-start(f32[4,4,128,128]{3,2,1,0:T(8,128)} %add.197), channel_id=1, source_target_pairs={{0,4},{4,8},{8,12},{12,16},{16,20},{20,24},{24,28},{28,0},{1,5},{5... | collective-permute-start | bytes 3145736 | tf_op jit(solution)/shard_map/while/body/eval_jaxpr/ppermute | solution.py:16
  659.7 25.5 %collective-permute-start = (bf16[4,4,128,128]{3,2,1,0:T(8,128)(2,1)}, bf16[4,4,128,128]{3,2,1,0:T(8,128)(2,1)S(1)}, u32[]{:S(2)}, u32[]{:S(2)}) collective-permute-start(bf16[4,4,128,128]{3,2,1,0:T(8,128)(2,1)} %get-tuple-element.557), channel_id=1, source_target_pairs={{0,4},{4,8},{8,12},{12,16},{16,20},{20,24},{24,28},{28,0},{1,5},{5... | collective-permute-start | bytes 1572872 | tf_op jit(solution)/shard_map/while/body/eval_jaxpr/ppermute | solution.py:16
where the time goes:
time: 701 us; the launch traced here: 690 us
  waiting for transfers between devices  220 us (31%)
  other arithmetic  184 us (26%)
  local copies, waits for them, and re-layouts  181 us (26%)
  matrix products  61.5 us (9%)
  blocking collectives  36.4 us (5%)
    ppermute x16, waiting for transfers between devices, from_behind(): lax.ppermute(array, axis, [(i, (i + by) % devices) for i in range(devices)])  220 us
    reduce_or x32, other arithmetic, tile_residual(): jnp.any(positives[:, :, None] == label_ids[None, None, :], axis=1)  126 us
    gather x32, local copies, waits for them, and re-layouts, one_block(): chosen = jnp.take(tile_split, block_rows, axis=1)  111 us
    dot_general x32, matrix products, one_block(): jnp.einsum('rsk,rt->skt', chosen, block_resid, preferred_element_type=jnp...  61.5 us
    dynamic_slice x64, local copies, waits for them, and re-layouts, block_both(): return lax.map(one_block, (row_ids, slot_counts, tiles_now, label_base))  42.6 us
    all_gather x1, blocking collectives, local(): lax.all_gather(tile_rows, 'blk', axis=0, tiled=True)  25.9 us
    and x32, other arithmetic, one_block(): chosen = jnp.take(tile_split, block_rows, axis=1)  22.4 us
    add x32, other arithmetic, tile_residual(): label_ids = block_base + jnp.arange(tile_side, dtype=jnp.int32)  22.1 us
  transfers between devices with their start and end apart: 16, of which 8 were waited for; matrix products, arithmetic and copies ran while one was open for 0% of the time, Pallas kernels for 0%

commit v1 on v0

v1 whole, which is shorter than its diff:
```python
import functools

import jax
import jax.numpy as jnp
from jax import lax
from jax.experimental import pallas as pl
from jax.experimental.pallas import tpu as pltpu
from jax.sharding import PartitionSpec as P

beta_one = 0.9
beta_two = 0.999
adam_eps = 1e-08
learn_rate = 0.1
correction_one = 1.0 - 0.9**10
correction_two = 1.0 - 0.999**10

F32 = jnp.float32
BF16 = jnp.bfloat16


def grad_kernel(
    blk, labels, own, slots, side, chunks,
    feat_in, tiles, pos, meta,
    grad,
    feat, feat2, pos2, tiles_in, meta_in, rows_s, acc, acc_in,
    y_send, y_recv, p_sem, x_send, x_recv, t_send, t_recv, m_send, m_recv, s_sem, g_send, g_recv, f_sem,
):
    me = lax.axis_index("blk")
    lab = lax.axis_index("labels")
    ring = blk // 2
    zed, par = me // 2, lax.rem(me, 2)
    partner = zed * 2 + (1 - par)
    cols, row_total, _ = feat.shape
    part = row_total // labels
    sub = part // chunks
    bits = []
    while (1 << len(bits)) < labels:
        bits.append(1 << len(bits))
    bits = bits[::-1]

    def at(k):
        return lax.rem(zed + k, ring) * 2 + par

    def flip(index, bit):
        return index + bit * (1 - 2 * lax.rem(index // bit, 2))

    def flip_all(mask):
        index = lab
        for bit in bits:
            if mask & bit:
                index = flip(index, bit)
        return index

    loads = [
        pltpu.make_async_copy(feat_in.at[:, pl.ds(j * side, side)], feat.at[j], f_sem.at[j])
        for j in range(cols)
    ]
    for load in loads:
        load.start()
    barrier = pltpu.get_barrier_semaphore()
    peers = [{"blk": partner}] + [{"blk": at(k)} for k in range(1, ring)]
    peers += [{"labels": flip(lab, bit)} for bit in bits]
    for peer in peers:
        pl.semaphore_signal(barrier, inc=1, device_id=peer, device_id_type=pl.DeviceIdType.MESH)
    pl.semaphore_wait(barrier, len(peers))

    def remote(src, dst, send, recv, peer):
        return pltpu.make_async_remote_copy(
            src_ref=src, dst_ref=dst, send_sem=send, recv_sem=recv,
            device_id=peer, device_id_type=pl.DeviceIdType.MESH,
        )

    def rows_of(mask, c):
        start = pl.multiple_of(flip_all(mask) * part + c * sub, 16)
        return pl.ds(start, sub)

    m_out, t_out = {}, {}
    for k in range(1, ring):
        m_out[k] = remote(meta, meta_in.at[k], m_send.at[k], m_recv.at[k], {"blk": at(k)})
        m_out[k].start()
    for load in loads:
        load.wait()
    y_out = []
    p_out = remote(pos, pos2, p_sem.at[0], p_sem.at[1], {"blk": partner})
    p_out.start()
    for c in range(chunks):
        rows = rows_of(0, c)
        y_out.append(remote(feat.at[:, rows], feat2.at[:, rows], y_send.at[c], y_recv.at[c], {"blk": partner}))
        y_out[c].start()
    for k in range(1, ring):
        t_out[k] = remote(tiles, tiles_in.at[k], t_send.at[k], t_recv.at[k], {"blk": at(k)})
        t_out[k].start()
    own_rows = pltpu.make_async_copy(meta, rows_s.at[0], s_sem.at[0])
    own_rows.start()
    own_rows.wait()

    x_out = {}

    def masks_before(step):
        found = [0]
        for bit in bits[:step]:
            found = found + [m | bit for m in found]
        return found

    def send_on(step, mask, c):
        slot = (mask | bits[step], c)
        sem = slot[0] * chunks + c
        rows = rows_of(mask, c)
        x_out[slot] = remote(
            feat2.at[:, rows], feat2.at[:, rows], x_send.at[sem], x_recv.at[sem],
            {"labels": flip(lab, bits[step])},
        )
        x_out[slot].start()

    def take_on(mask, c):
        sem = mask * chunks + c
        rows = rows_of(mask, c)
        pltpu.make_async_remote_copy(
            src_ref=feat2.at[:, rows], dst_ref=feat2.at[:, rows], send_sem=x_send.at[sem],
            recv_sem=x_recv.at[sem], device_id={"labels": flip(lab, mask & -mask)},
            device_id_type=pl.DeviceIdType.MESH,
        ).wait_recv()

    def relay(stage, c):
        if stage == 0:
            y_out[c].wait_recv()
            for step in range(len(bits)):
                send_on(step, 0, c)
            return
        low = bits[stage - 1]
        for m in masks_before(stage - 1):
            take_on(m | low, c)
            for step in range(stage, len(bits)):
                send_on(step, m | low, c)

    label_iota = lax.broadcasted_iota(jnp.int32, (side, 1), 0)
    step_rows = 256 if row_total % 256 == 0 else row_total

    def owner_pass(slab, slab_pos, k, tile_ref, first):
        owner = lax.rem(zed - k + ring, ring) * 2 + par
        base = (lab * blk + owner) * own * side

        def block(b, _):
            wt = tile_ref[b]
            ids = base + b * side + label_iota
            at_rows = [rows_s[k, 0, b * slots + s] for s in range(slots)]
            total = None
            for r in range(0, row_total, step_rows):
                chosen = jnp.concatenate(
                    [slab[col, r:r + step_rows, :] for col in at_rows], axis=1
                )
                logits = lax.dot_general(
                    wt, chosen, (((1,), (1,)), ((), ())), preferred_element_type=F32
                )
                hit = None
                for p in range(slab_pos.shape[0]):
                    same = slab_pos[p:p + 1, r:r + step_rows] == ids
                    hit = same if hit is None else hit | same
                resid = (jax.nn.sigmoid(logits) - jnp.where(hit, 1.0, 0.0)).astype(BF16)
                term = jnp.dot(resid, chosen, preferred_element_type=F32)
                total = term if total is None else total + term
            if first:
                acc[k, b] = total
            else:
                acc[k, b] += total
            return 0

        lax.fori_loop(0, own, block, 0)

    stages = len(bits) + 1
    todo = sorted(((c + s, s, c) for c in range(chunks) for s in range(stages)), key=lambda x: (x[0], x[1]))
    todo = [(s, c) for _, s, c in todo]
    share = max(1, len(todo) // (ring + 1))

    owner_pass(feat, pos, 0, tiles, True)
    for k in range(1, ring):
        for _ in range(share):
            relay(*todo.pop(0))
        m_out[k].wait_recv()
        t_out[k].wait_recv()
        row_copy = pltpu.make_async_copy(meta_in.at[k], rows_s.at[k], s_sem.at[k])
        row_copy.start()
        row_copy.wait()
        owner_pass(feat, pos, k, tiles_in.at[k], True)
    while todo:
        relay(*todo.pop(0))
    p_out.wait_recv()

    g_out = {}
    for k in list(range(1, ring)):
        owner_pass(feat2, pos2, k, tiles_in.at[k], False)
        g_out[k] = remote(
            acc.at[k], acc_in.at[k], g_send.at[k], g_recv.at[k],
            {"blk": lax.rem(zed - k + ring, ring) * 2 + par},
        )
        g_out[k].start()
    owner_pass(feat2, pos2, 0, tiles, False)
    for k in range(1, ring):
        g_out[k].wait_recv()

    def finish(b, _):
        total = acc[0, b]
        for k in range(1, ring):
            total = total + acc_in[k, b]
        for s in range(slots):
            grad[b, s] = total[:, s * side:(s + 1) * side].T
        return 0

    lax.fori_loop(0, own, finish, 0)
    for k in range(1, ring):
        m_out[k].wait_send()
        t_out[k].wait_send()
        g_out[k].wait_send()
    p_out.wait_send()
    for c in range(chunks):
        y_out[c].wait_send()
    for copy in x_out.values():
        copy.wait_send()


def local(blk, labels, features, positives, tile_rows, tile_count, weight, first_moment, second_moment):
    own, slots, side, _ = weight.shape
    ring = blk // 2
    row_total = features.shape[0]
    cols = features.shape[1] // side
    slot_ids = jnp.arange(slots, dtype=jnp.int32)
    kept = (slot_ids[None, :] < tile_count[:, None])[:, :, None, None]
    masked = jnp.where(kept, weight, 0.0).astype(BF16)
    tiles = masked.transpose(0, 3, 1, 2).reshape(own, side, slots * side)
    meta = jnp.pad(tile_rows.reshape(1, own * slots), ((0, 7), (0, 128 - own * slots)))
    pos = positives.T
    part = row_total // labels
    chunks = next(c for c in (4, 3, 2, 1) if part % (16 * c) == 0)
    vmem = pl.BlockSpec(memory_space=pltpu.VMEM)
    dma = pltpu.SemaphoreType.DMA
    gradient = pl.pallas_call(
        functools.partial(grad_kernel, blk, labels, own, slots, side, chunks),
        out_shape=jax.ShapeDtypeStruct(weight.shape, F32),
        in_specs=[pl.BlockSpec(memory_space=pl.ANY)] + [vmem] * 3,
        out_specs=vmem,
        scratch_shapes=[
            pltpu.VMEM((cols, row_total, side), BF16),
            pltpu.VMEM((cols, row_total, side), BF16),
            pltpu.VMEM(pos.shape, jnp.int32),
            pltpu.VMEM((ring,) + tiles.shape, BF16),
            pltpu.VMEM((ring,) + meta.shape, jnp.int32),
            pltpu.SMEM((ring,) + meta.shape, jnp.int32),
            pltpu.VMEM((ring,) + tiles.shape, F32),
            pltpu.VMEM((ring,) + tiles.shape, F32),
            dma((chunks,)), dma((chunks,)), dma((2,)),
            dma((labels * chunks,)), dma((labels * chunks,)),
            dma((ring,)), dma((ring,)), dma((ring,)), dma((ring,)), dma((ring,)),
            dma((ring,)), dma((ring,)), dma((cols,)),
        ],
        compiler_params=pltpu.CompilerParams(collective_id=0, has_side_effects=True),
    )(features, tiles, pos, meta)
    moved_first = beta_one * first_moment + (1.0 - beta_one) * gradient
    moved_second = beta_two * second_moment + (1.0 - beta_two) * gradient * gradient
    step_dir = moved_first / correction_one / (jnp.sqrt(moved_second / correction_two) + adam_eps)
    moved_weight = weight - learn_rate * step_dir
    new_weight = jnp.where(kept, moved_weight, weight)
    new_first = jnp.where(kept, moved_first, first_moment)
    new_second = jnp.where(kept, moved_second, second_moment)
    return (new_weight, new_first, new_second)


def solution(mesh):
    owner = P(("labels", "blk"), None, None, None)
    return jax.shard_map(
        functools.partial(local, mesh.shape["blk"], mesh.shape["labels"]),
        mesh=mesh,
        in_specs=(
            P("blk", None),
            P("blk", None),
            P(("labels", "blk"), None),
            P(("labels", "blk")),
            owner, owner, owner,
        ),
        out_specs=(owner, owner, owner),
        check_vma=False,
    )
```

time: 701 us -> 171 us (0.24)
  the two profiles are of different devices: /device:TPU:8 before, /device:TPU:1 now
where the time goes in v1:
time: 171 us
  Pallas kernels  162 us (95%)
  other arithmetic  6.16 us (4%)
  local copies, waits for them, and re-layouts  2.39 us (1%)
    pallas_call x1, Pallas kernels, local(): pl.pallas_call(functools.partial(grad_kernel, blk, labels, own, slots, si...  162 us
    select_n x1, other arithmetic, local(): new_second = jnp.where(kept, moved_second, second_moment)  3.9 us

profile of v1, /device:TPU:1, one launch (start us, length us, event | category | flops | bytes accessed | tf_op | source)
XLA Modules:
  0.0 171.2 jit_solution(14751125174552060677)
XLA Ops:
  0.6 0.0 copy-start
  0.6 0.0 copy-start.1
  0.7 0.9 iota_compare_fusion
  1.5 0.8 reshape.34
  2.3 0.6 pad.4.meta
  2.9 1.4 select_convert_fusion
  4.3 1.0 copy.11.tiles
  5.3 0.0 copy-start.2
  5.3 161.9 %shard_map.94 = f32[4,4,128,128]{3,2,1,0:T(8,128)} custom-call(bf16[768,4096]{1,0:T(8,128)(2,1)} %feat_in.1, bf16[4,128,512]{2,1,0:T(8,128)(2,1)} %copy.11.tiles, s32[8,768]{1,0:T(8,128)} %bitcast.5, s32[8,128]{1,0:T(8,128)} %pad.4.meta), custom_call_target="tpu_custom_call" | custom-call | tf_op jit(solution)/shard_map/pallas_call | solution.py:236
  167.2 0.0 copy-done
  167.2 0.0 copy-done.1
  167.3 0.0 copy-done.2
  167.3 3.9 %fusion.2 = (f32[4,4,128,128]{3,2,1,0:T(8,128)}, f32[4,4,128,128]{3,2,1,0:T(8,128)}, f32[4,4,128,128]{3,2,1,0:T(8,128)}) fusion(f32[4,4,128,128]{3,2,1,0:T(8,128)S(1)} %copy-done.1, f32[4,4,128,128]{3,2,1,0:T(8,128)} %shard_map.94, pred[4,4]{1,0:T(4,128)(4,1)S(1)} %iota_compare_fusion, f32[4,4,128,128]{3,2,1,0:T(8,128)S(1)} %copy-done, ...), kind=kLoop, calls=%fused_computation.6 | loop fusion | flops 4194304 | bytes 7340048 | tf_op jit(solution)/shard_map/jit(_where)/select_n | solution.py:263
Async XLA Ops:
  0.6 166.6 %copy-start = (f32[4,4,128,128]{3,2,1,0:T(8,128)S(1)}, f32[4,4,128,128]{3,2,1,0:T(8,128)}, u32[]{:S(2)}) copy-start(f32[4,4,128,128]{3,2,1,0:T(8,128)} %param.11) | copy-start | bytes 3145732
  0.6 166.6 %copy-start.1 = (f32[4,4,128,128]{3,2,1,0:T(8,128)S(1)}, f32[4,4,128,128]{3,2,1,0:T(8,128)}, u32[]{:S(2)}) copy-start(f32[4,4,128,128]{3,2,1,0:T(8,128)} %param.13) | copy-start | bytes 3145732
  5.3 162.0 %copy-start.2 = (f32[4,4,128,128]{3,2,1,0:T(8,128)S(1)}, f32[4,4,128,128]{3,2,1,0:T(8,128)}, u32[]{:S(2)}) copy-start(f32[4,4,128,128]{3,2,1,0:T(8,128)} %param.12) | copy-start | bytes 3145732

commit v2 on v1

--- a/solution.py
+++ b/solution.py
@@ -74,10 +74,43 @@
         start = pl.multiple_of(flip_all(mask) * part + c * sub, 16)
         return pl.ds(start, sub)
 
-    m_out, t_out = {}, {}
+    m_out = {}
     for k in range(1, ring):
         m_out[k] = remote(meta, meta_in.at[k], m_send.at[k], m_recv.at[k], {"blk": at(k)})
         m_out[k].start()
+
+    def beside(way):
+        return {"blk": (zed + 1 - 2 * way) * 2 + par}
+
+    def tile_copy(way, d):
+        owner = zed - d + 2 * d * way
+        src = tiles if d == 0 else tiles_in.at[owner]
+        return remote(src, tiles_in.at[owner], t_send.at[way, d], t_recv.at[way, d + 1], beside(way))
+
+    def has(way, d):
+        return zed >= d if way == 0 else zed + d < ring
+
+    def sends_tile(way, d):
+        return has(way, d) & has(1 - way, 1)
+
+    def send_tile(way, d):
+        if d + 1 >= ring:
+            return
+
+        @pl.when(sends_tile(way, d))
+        def _():
+            tile_copy(way, d).start()
+
+    def take_tile(way, d):
+        @pl.when(has(way, d))
+        def _():
+            owner = zed - d + 2 * d * way
+            remote(
+                tiles_in.at[owner], tiles_in.at[owner], t_send.at[way, d], t_recv.at[way, d], beside(way)
+            ).wait_recv()
+
+    for way in range(2):
+        send_tile(way, 0)
     for load in loads:
         load.wait()
     y_out = []
@@ -87,10 +120,7 @@
         rows = rows_of(0, c)
         y_out.append(remote(feat.at[:, rows], feat2.at[:, rows], y_send.at[c], y_recv.at[c], {"blk": partner}))
         y_out[c].start()
-    for k in range(1, ring):
-        t_out[k] = remote(tiles, tiles_in.at[k], t_send.at[k], t_recv.at[k], {"blk": at(k)})
-        t_out[k].start()
-    own_rows = pltpu.make_async_copy(meta, rows_s.at[0], s_sem.at[0])
+    own_rows = pltpu.make_async_copy(meta, rows_s.at[zed], s_sem.at[0])
     own_rows.start()
     own_rows.wait()
 
@@ -136,14 +166,12 @@
     label_iota = lax.broadcasted_iota(jnp.int32, (side, 1), 0)
     step_rows = 256 if row_total % 256 == 0 else row_total
 
-    def owner_pass(slab, slab_pos, k, tile_ref, first):
-        owner = lax.rem(zed - k + ring, ring) * 2 + par
-        base = (lab * blk + owner) * own * side
-
-        def block(b, _):
+    def one_block(slab, slab_pos, owner, tile_ref, first, b):
+        base = (lab * blk + owner * 2 + par) * own * side
+        if True:
             wt = tile_ref[b]
             ids = base + b * side + label_iota
-            at_rows = [rows_s[k, 0, b * slots + s] for s in range(slots)]
+            at_rows = [rows_s[owner, 0, b * slots + s] for s in range(slots)]
             total = None
             for r in range(0, row_total, step_rows):
                 chosen = jnp.concatenate(
@@ -160,48 +188,87 @@
                 term = jnp.dot(resid, chosen, preferred_element_type=F32)
                 total = term if total is None else total + term
             if first:
-                acc[k, b] = total
+                acc[owner, b] = total
             else:
-                acc[k, b] += total
+                acc[owner, b] += total
+
+    def owner_pass(slab, slab_pos, owner, tile_ref, first):
+        def block(b, _):
+            one_block(slab, slab_pos, owner, tile_ref, first, b)
             return 0
 
         lax.fori_loop(0, own, block, 0)
 
     stages = len(bits) + 1
     todo = sorted(((c + s, s, c) for c in range(chunks) for s in range(stages)), key=lambda x: (x[0], x[1]))
-    todo = [(s, c) for _, s, c in todo]
-    share = max(1, len(todo) // (ring + 1))
-
-    owner_pass(feat, pos, 0, tiles, True)
+    def relay_next():
+        now = todo[0][0] if todo else None
+        while todo and todo[0][0] == now:
+            _, stage, c = todo.pop(0)
+            relay(stage, c)
+
+    owner_pass(feat, pos, zed, tiles, True)
     for k in range(1, ring):
-        for _ in range(share):
-            relay(*todo.pop(0))
         m_out[k].wait_recv()
-        t_out[k].wait_recv()
-        row_copy = pltpu.make_async_copy(meta_in.at[k], rows_s.at[k], s_sem.at[k])
+        row_copy = pltpu.make_async_copy(
+            meta_in.at[k], rows_s.at[lax.rem(zed - k + ring, ring)], s_sem.at[k]
+        )
         row_copy.start()
         row_copy.wait()
-        owner_pass(feat, pos, k, tiles_in.at[k], True)
+    relay_next()
+    for d in range(1, ring):
+        for way in range(2):
+            take_tile(way, d)
+            send_tile(way, d)
+        for way in range(2):
+            @pl.when(has(way, d))
+            def _():
+                owner = zed - d + 2 * d * way
+                owner_pass(feat, pos, owner, tiles_in.at[owner], True)
+
+            relay_next()
     while todo:
-        relay(*todo.pop(0))
+        relay_next()
     p_out.wait_recv()
 
-    g_out = {}
-    for k in list(range(1, ring)):
-        owner_pass(feat2, pos2, k, tiles_in.at[k], False)
-        g_out[k] = remote(
-            acc.at[k], acc_in.at[k], g_send.at[k], g_recv.at[k],
-            {"blk": lax.rem(zed - k + ring, ring) * 2 + par},
+    def sum_copy(way, owner, b):
+        return remote(
+            acc.at[owner, b], acc_in.at[way, owner, b],
+            g_send.at[way, owner, b], g_recv.at[way, owner, b], beside(way),
         )
-        g_out[k].start()
-    owner_pass(feat2, pos2, 0, tiles, False)
-    for k in range(1, ring):
-        g_out[k].wait_recv()
+
+    def passes(way, step):
+        owner = ring - 1 - step if way == 0 else step
+        return owner, (zed < owner if way == 0 else zed > owner)
+
+    for step in range(ring - 1):
+        def hop(b, _):
+            for way in range(2):
+                owner, goes = passes(way, step)
+
+                @pl.when(goes)
+                def _():
+                    one_block(feat2, pos2, owner, tiles_in.at[owner], False, b)
+
+                    @pl.when(has(way, 1))
+                    def _():
+                        sum_copy(way, owner, b).wait_recv()
+                        acc[owner, b] += acc_in[way, owner, b]
+
+                    sum_copy(way, owner, b).start()
+            return 0
+
+        lax.fori_loop(0, own, hop, 0)
+    owner_pass(feat2, pos2, zed, tiles, False)
 
     def finish(b, _):
-        total = acc[0, b]
-        for k in range(1, ring):
-            total = total + acc_in[k, b]
+        for way in range(2):
+            @pl.when(has(way, 1))
+            def _():
+                sum_copy(way, zed, b).wait_recv()
+                acc[zed, b] += acc_in[way, zed, b]
+
+        total = acc[zed, b]
         for s in range(slots):
             grad[b, s] = total[:, s * side:(s + 1) * side].T
         return 0
@@ -209,8 +276,21 @@
     lax.fori_loop(0, own, finish, 0)
     for k in range(1, ring):
         m_out[k].wait_send()
-        t_out[k].wait_send()
-        g_out[k].wait_send()
+    for way in range(2):
+        for d in range(ring - 1):
+            @pl.when(sends_tile(way, d))
+            def _():
+                tile_copy(way, d).wait_send()
+        for step in range(ring - 1):
+            owner, goes = passes(way, step)
+
+            @pl.when(goes)
+            def _():
+                def sent(b, _):
+                    sum_copy(way, owner, b).wait_send()
+                    return 0
+
+                lax.fori_loop(0, own, sent, 0)
     p_out.wait_send()
     for c in range(chunks):
         y_out[c].wait_send()
@@ -230,7 +310,7 @@
     meta = jnp.pad(tile_rows.reshape(1, own * slots), ((0, 7), (0, 128 - own * slots)))
     pos = positives.T
     part = row_total // labels
-    chunks = next(c for c in (4, 3, 2, 1) if part % (16 * c) == 0)
+    chunks = next(c for c in (6, 4, 3, 2, 1) if part % (16 * c) == 0)
     vmem = pl.BlockSpec(memory_space=pltpu.VMEM)
     dma = pltpu.SemaphoreType.DMA
     gradient = pl.pallas_call(
@@ -246,11 +326,11 @@
             pltpu.VMEM((ring,) + meta.shape, jnp.int32),
             pltpu.SMEM((ring,) + meta.shape, jnp.int32),
             pltpu.VMEM((ring,) + tiles.shape, F32),
-            pltpu.VMEM((ring,) + tiles.shape, F32),
+            pltpu.VMEM((2, ring) + tiles.shape, F32),
             dma((chunks,)), dma((chunks,)), dma((2,)),
             dma((labels * chunks,)), dma((labels * chunks,)),
-            dma((ring,)), dma((ring,)), dma((ring,)), dma((ring,)), dma((ring,)),
-            dma((ring,)), dma((ring,)), dma((cols,)),
+            dma((2, ring)), dma((2, ring)), dma((ring,)), dma((ring,)), dma((ring,)),
+            dma((2, ring, own)), dma((2, ring, own)), dma((cols,)),
         ],
         compiler_params=pltpu.CompilerParams(collective_id=0, has_side_effects=True),
     )(features, tiles, pos, meta)

time: 171 us -> 152 us (0.89)
  the two profiles are of different devices: /device:TPU:1 before, /device:TPU:8 now
where the time goes in v2:
time: 152 us
  Pallas kernels  143 us (94%)
  other arithmetic  6.16 us (4%)
  local copies, waits for them, and re-layouts  2.39 us (2%)
    pallas_call x1, Pallas kernels, local(): pl.pallas_call(functools.partial(grad_kernel, blk, labels, own, slots, si...  143 us
    select_n x1, other arithmetic, local(): new_second = jnp.where(kept, moved_second, second_moment)  3.9 us

profile of v2, /device:TPU:8, one launch (start us, length us, event | category | flops | bytes accessed | tf_op | source)
XLA Modules:
  0.0 152.1 jit_solution(17355322493558438939)
XLA Ops:
  0.6 0.0 copy-start
  0.6 0.0 copy-start.1
  0.7 0.9 iota_compare_fusion
  1.5 0.8 reshape.34
  2.3 0.6 pad.4.meta
  2.9 1.4 select_convert_fusion
  4.3 1.0 copy.11.tiles
  5.3 0.0 copy-start.2
  5.3 142.9 %shard_map.94 = f32[4,4,128,128]{3,2,1,0:T(8,128)} custom-call(bf16[768,4096]{1,0:T(8,128)(2,1)} %feat_in.1, bf16[4,128,512]{2,1,0:T(8,128)(2,1)} %copy.11.tiles, s32[8,768]{1,0:T(8,128)} %bitcast.5, s32[8,128]{1,0:T(8,128)} %pad.4.meta), custom_call_target="tpu_custom_call" | custom-call | tf_op jit(solution)/shard_map/pallas_call | solution.py:316
  148.2 0.0 copy-done
  148.2 0.0 copy-done.1
  148.2 0.0 copy-done.2
  148.2 3.9 %fusion.2 = (f32[4,4,128,128]{3,2,1,0:T(8,128)}, f32[4,4,128,128]{3,2,1,0:T(8,128)}, f32[4,4,128,128]{3,2,1,0:T(8,128)}) fusion(f32[4,4,128,128]{3,2,1,0:T(8,128)S(1)} %copy-done.1, f32[4,4,128,128]{3,2,1,0:T(8,128)} %shard_map.94, pred[4,4]{1,0:T(4,128)(4,1)S(1)} %iota_compare_fusion, f32[4,4,128,128]{3,2,1,0:T(8,128)S(1)} %copy-done, ...), kind=kLoop, calls=%fused_computation.6 | loop fusion | flops 4194304 | bytes 7340048 | tf_op jit(solution)/shard_map/jit(_where)/select_n | solution.py:343
Async XLA Ops:
  0.6 147.5 %copy-start = (f32[4,4,128,128]{3,2,1,0:T(8,128)S(1)}, f32[4,4,128,128]{3,2,1,0:T(8,128)}, u32[]{:S(2)}) copy-start(f32[4,4,128,128]{3,2,1,0:T(8,128)} %param.11) | copy-start | bytes 3145732
  0.6 147.5 %copy-start.1 = (f32[4,4,128,128]{3,2,1,0:T(8,128)S(1)}, f32[4,4,128,128]{3,2,1,0:T(8,128)}, u32[]{:S(2)}) copy-start(f32[4,4,128,128]{3,2,1,0:T(8,128)} %param.13) | copy-start | bytes 3145732
  5.3 142.9 %copy-start.2 = (f32[4,4,128,128]{3,2,1,0:T(8,128)S(1)}, f32[4,4,128,128]{3,2,1,0:T(8,128)}, u32[]{:S(2)}) copy-start(f32[4,4,128,128]{3,2,1,0:T(8,128)} %param.12) | copy-start | bytes 3145732

commit v3 on v2

--- a/solution.py
+++ b/solution.py
@@ -310,7 +310,7 @@
     meta = jnp.pad(tile_rows.reshape(1, own * slots), ((0, 7), (0, 128 - own * slots)))
     pos = positives.T
     part = row_total // labels
-    chunks = next(c for c in (6, 4, 3, 2, 1) if part % (16 * c) == 0)
+    chunks = next(c for c in (12, 6, 4, 3, 2, 1) if part % (16 * c) == 0)
     vmem = pl.BlockSpec(memory_space=pltpu.VMEM)
     dma = pltpu.SemaphoreType.DMA
     gradient = pl.pallas_call(

time: 152 us -> 166 us (1.092)
  Pallas kernels: 143 us -> 157 us
    pallas_call x1, Pallas kernels: 143 us -> 157 us  [local(): pl.pallas_call(functools.partial(grad_kernel, blk, labels, own, slots, si...]
where the time goes in v3:
time: 166 us
  Pallas kernels  157 us (95%)
  other arithmetic  6.16 us (4%)
  local copies, waits for them, and re-layouts  2.39 us (1%)
    pallas_call x1, Pallas kernels, local(): pl.pallas_call(functools.partial(grad_kernel, blk, labels, own, slots, si...  157 us
    select_n x1, other arithmetic, local(): new_second = jnp.where(kept, moved_second, second_moment)  3.9 us

profile of v3, /device:TPU:8, one launch (start us, length us, event | category | flops | bytes accessed | tf_op | source)
XLA Modules:
  0.0 165.8 jit_solution(7233812275164931724)
XLA Ops:
  0.6 0.0 copy-start
  0.6 0.0 copy-start.1
  0.7 0.9 iota_compare_fusion
  1.5 0.8 reshape.34
  2.3 0.6 pad.4.meta
  2.9 1.4 select_convert_fusion
  4.3 1.0 copy.11.tiles
  5.3 0.0 copy-start.2
  5.3 156.6 %shard_map.94 = f32[4,4,128,128]{3,2,1,0:T(8,128)} custom-call(bf16[768,4096]{1,0:T(8,128)(2,1)} %feat_in.1, bf16[4,128,512]{2,1,0:T(8,128)(2,1)} %copy.11.tiles, s32[8,768]{1,0:T(8,128)} %bitcast.5, s32[8,128]{1,0:T(8,128)} %pad.4.meta), custom_call_target="tpu_custom_call" | custom-call | tf_op jit(solution)/shard_map/pallas_call | solution.py:316
  161.9 0.0 copy-done
  161.9 0.0 copy-done.1
  161.9 0.0 copy-done.2
  161.9 3.9 %fusion.2 = (f32[4,4,128,128]{3,2,1,0:T(8,128)}, f32[4,4,128,128]{3,2,1,0:T(8,128)}, f32[4,4,128,128]{3,2,1,0:T(8,128)}) fusion(f32[4,4,128,128]{3,2,1,0:T(8,128)S(1)} %copy-done.1, f32[4,4,128,128]{3,2,1,0:T(8,128)} %shard_map.94, pred[4,4]{1,0:T(4,128)(4,1)S(1)} %iota_compare_fusion, f32[4,4,128,128]{3,2,1,0:T(8,128)S(1)} %copy-done, ...), kind=kLoop, calls=%fused_computation.6 | loop fusion | flops 4194304 | bytes 7340048 | tf_op jit(solution)/shard_map/jit(_where)/select_n | solution.py:343
Async XLA Ops:
  0.6 161.2 %copy-start = (f32[4,4,128,128]{3,2,1,0:T(8,128)S(1)}, f32[4,4,128,128]{3,2,1,0:T(8,128)}, u32[]{:S(2)}) copy-start(f32[4,4,128,128]{3,2,1,0:T(8,128)} %param.11) | copy-start | bytes 3145732
  0.6 161.2 %copy-start.1 = (f32[4,4,128,128]{3,2,1,0:T(8,128)S(1)}, f32[4,4,128,128]{3,2,1,0:T(8,128)}, u32[]{:S(2)}) copy-start(f32[4,4,128,128]{3,2,1,0:T(8,128)} %param.13) | copy-start | bytes 3145732
  5.3 156.6 %copy-start.2 = (f32[4,4,128,128]{3,2,1,0:T(8,128)S(1)}, f32[4,4,128,128]{3,2,1,0:T(8,128)}, u32[]{:S(2)}) copy-start(f32[4,4,128,128]{3,2,1,0:T(8,128)} %param.12) | copy-start | bytes 3145732
